TPU v7x, 32 devices: a whole 2x2x4 slice. The times are simulated.
32 devices in a mesh: req: 4 (over y, x), mlp: 8 (over z, core).
Axes of the slice: x: 2, y: 2, z: 4, core: 2. Of those that a mesh axis runs over, the one named last changes fastest.
Arguments:
- tokens: bfloat16 [64, 4608], P(('req', 'mlp')), may hold values from -6 to 6
- segments: int32 [4, 16], replicated, may hold values from 0 to 3, never falling along the last dimension, each value on 1 to 8 neighbouring positions
- owners: int32 [4], replicated, may hold values from 0 to 3, each once
- sink_keys: bfloat16 [4, 2048], P(None, 'mlp'), may hold values from -21 to 21
- sink_values: bfloat16 [4, 2048], P(None, 'mlp'), may hold values from -6 to 6
- window_keys: bfloat16 [4096, 2048], P('req', 'mlp'), may hold values from -6 to 6
- window_values: bfloat16 [4096, 2048], P('req', 'mlp'), may hold values from -6 to 6
- attn_gain: float32 [4608], replicated, may hold values from 0.1 to 1.9
- post_attn_gain: float32 [4608], replicated, may hold values from 0.1 to 1.9
- ffn_gain: float32 [4608], replicated, may hold values from 0.1 to 1.9
- post_ffn_gain: float32 [4608], replicated, may hold values from 0.1 to 1.9
- w_query: bfloat16 [4608, 4096], P(None, 'mlp'), may hold values from -0.09375 to 0.09375
- w_key: bfloat16 [4608, 2048], P(None, 'mlp'), may hold values from -0.25 to 0.25
- w_value: bfloat16 [4608, 2048], P(None, 'mlp'), may hold values from -0.09375 to 0.09375
- w_out: bfloat16 [4096, 4608], P('mlp'), may hold values from -0.09375 to 0.09375
- w_gate: bfloat16 [36864, 4608], P(('req', 'mlp')), may hold values from -0.09375 to 0.09375
- w_up: bfloat16 [36864, 4608], P(('req', 'mlp')), may hold values from -0.09375 to 0.09375
- w_down: bfloat16 [36864, 4608], P(('req', 'mlp')), may hold values from -0.03125 to 0.03125
Outputs:
- mixed: bfloat16 [64, 4608], P(('req', 'mlp'))
Inputs may be any that keep to these rules, and one draw needn't show every extreme that they name: `segments`: row g gives, for the 16 suffix tokens of request group g in order, which of the group's 4 requests each belongs to; a request's tokens are contiguous and its number never falls along the row. Req index d holds array rows d * B to d * B + B - 1 of window_keys and window_values, whose window positions are owners[d] * B to owners[d] * B + B - 1, B = 4096 / 4; every block of positions is held once.
All inputs are finite; a program needn't handle non-finite values.
Results may differ from a plain program's by a relative error of at most 0.015.
Values may be sent and summed in bfloat16 or wider, within the bound.
A program may use at most 128 MiB of HBM per device.

v0:
```python
import jax
import jax.numpy as jnp
from jax import lax
from jax.sharding import PartitionSpec as P

HEADS = 32
KVH = 16
HD = 128
SINK = 4
GTOK = 16
epsilon = 1e-06
soft_cap = 50.0
logit_scale = 1.0 / 12.0


def rms_scale(values):
    return values * lax.rsqrt(jnp.mean(values * values, axis=-1, keepdims=True) + epsilon)


def positions(seg_rows):
    ordering = jnp.arange(seg_rows.shape[-1], dtype=jnp.int32)
    same_seg = seg_rows[..., :, None] == seg_rows[..., None, :]
    earlier = ordering[None, :] < ordering[:, None]
    return jnp.sum((same_seg & earlier).astype(jnp.int32), axis=-1)


def lookup(entries, indices):
    slots = jnp.arange(entries.shape[0], dtype=jnp.int32)
    return jnp.sum(jnp.where(indices[:, None] == slots[None, :], entries[None, :], 0), axis=1)


def attend(query_rows, key_matrix_rows, value_matrix_rows, visible):
    score_matrix = (
        jnp.einsum(
            "woji,roi->wojr", query_rows, key_matrix_rows, preferred_element_type=jnp.float32
        )
        * logit_scale
    )
    weight = jnp.exp(soft_cap * jnp.tanh(score_matrix / soft_cap))
    weight = jnp.where(visible[:, None, None, :], weight, 0.0)
    totals = jnp.sum(weight, axis=-1)
    summed_output = jnp.einsum(
        "xfka,afq->xfkq",
        weight.astype(jnp.bfloat16),
        value_matrix_rows,
        preferred_element_type=jnp.float32,
    )
    return (summed_output, totals)


def shards(
    tokens,
    segments,
    owners,
    sink_keys,
    sink_values,
    window_keys,
    window_values,
    attn_gain,
    post_attn_gain,
    ffn_gain,
    post_ffn_gain,
    w_query,
    w_key,
    w_value,
    w_out,
    w_gate,
    w_up,
    w_down,
):
    per_kv = HEADS // KVH
    local_heads = w_key.shape[1] // HD
    token_float = tokens.astype(jnp.float32)
    normed = (rms_scale(token_float) * attn_gain).astype(jnp.bfloat16)
    group_rows = lax.all_gather(normed, "mlp", axis=0, tiled=True)
    query_rows = (
        jnp.dot(group_rows, w_query, preferred_element_type=jnp.float32)
        .astype(jnp.bfloat16)
        .reshape(GTOK, local_heads, per_kv, HD)
    )
    key_new = (
        jnp.dot(group_rows, w_key, preferred_element_type=jnp.float32)
        .astype(jnp.bfloat16)
        .reshape(GTOK, local_heads, HD)
    )
    value_new = (
        jnp.dot(group_rows, w_value, preferred_element_type=jnp.float32)
        .astype(jnp.bfloat16)
        .reshape(GTOK, local_heads, HD)
    )
    req_index = lax.axis_index("req")
    pos_all = positions(segments)
    pos_row = lax.dynamic_index_in_dim(pos_all, req_index, 0, keepdims=False)
    seg_row = lax.dynamic_index_in_dim(segments, req_index, 0, keepdims=False)
    sink_key = sink_keys.reshape(SINK, local_heads, HD)
    sink_value = sink_values.reshape(SINK, local_heads, HD)
    sink_sum, sink_tot = attend(
        query_rows, sink_key, sink_value, jnp.ones((GTOK, SINK), dtype=jnp.bool_)
    )
    ordering = jnp.arange(GTOK, dtype=jnp.int32)
    local_vis = (seg_row[:, None] == seg_row[None, :]) & (ordering[None, :] <= ordering[:, None])
    loc_sum, loc_tot = attend(query_rows, key_new, value_new, local_vis)
    block_rows = window_keys.shape[0]
    piece_key = lax.all_gather(window_keys, "req", axis=0, tiled=True).reshape(-1, local_heads, HD)
    piece_value = lax.all_gather(window_values, "req", axis=0, tiled=True).reshape(
        -1, local_heads, HD
    )
    row_ids = jnp.arange(piece_key.shape[0], dtype=jnp.int32)
    window_pos = lookup(owners, row_ids // block_rows) * block_rows + row_ids % block_rows
    part_sum, part_tot = attend(
        query_rows, piece_key, piece_value, window_pos[None, :] > pos_row[:, None]
    )
    merged = (sink_sum + part_sum + loc_sum) / (sink_tot + part_tot + loc_tot)[..., None]
    attended = merged.astype(jnp.bfloat16).reshape(GTOK, local_heads * per_kv * HD)
    projected = jnp.dot(attended, w_out, preferred_element_type=jnp.float32)
    head_total = lax.psum_scatter(
        projected.astype(jnp.bfloat16), "mlp", scatter_dimension=0, tiled=True
    ).astype(jnp.float32)
    residual = token_float + rms_scale(head_total) * post_attn_gain
    ffn_in = (rms_scale(residual) * ffn_gain).astype(jnp.bfloat16)
    contract = (((1,), (1,)), ((), ()))
    piece = lax.all_gather(ffn_in, ("req", "mlp"), axis=0, tiled=True)
    gate_part = lax.dot_general(piece, w_gate, contract, preferred_element_type=jnp.float32)
    up_part = lax.dot_general(piece, w_up, contract, preferred_element_type=jnp.float32)
    hidden = (jax.nn.gelu(gate_part, approximate=True) * up_part).astype(jnp.bfloat16)
    ffn_out = lax.psum_scatter(
        jnp.dot(hidden, w_down, preferred_element_type=jnp.float32),
        ("req", "mlp"),
        scatter_dimension=0,
        tiled=True,
    )
    return (residual + rms_scale(ffn_out) * post_ffn_gain).astype(jnp.bfloat16)


def solution(mesh):
    return jax.shard_map(
        shards,
        mesh=mesh,
        in_specs=(
            P(("req", "mlp"), None),
            P(),
            P(),
            P(None, "mlp"),
            P(None, "mlp"),
            P("req", "mlp"),
            P("req", "mlp"),
            P(),
            P(),
            P(),
            P(),
            P(None, "mlp"),
            P(None, "mlp"),
            P(None, "mlp"),
            P("mlp", None),
            P(("req", "mlp"), None),
            P(("req", "mlp"), None),
            P(("req", "mlp"), None),
        ),
        out_specs=P(("req", "mlp"), None),
        check_vma=False,
    )
```

profile of v0, /device:TPU:0, one launch (start us, length us, event | category | flops | bytes accessed | tf_op | source)
XLA Modules:
  0.0 348.4 jit_solution(10756203467283247268)
XLA Ops:
  6.5 0.0 copy-start
  6.5 0.0 all-gather.5.cloned.1.call-start
  6.5 2.2 copy.56
  8.8 0.0 all-gather.5.cloned.1.call-update
  8.8 0.0 all-gather.7.cloned.1.call-start
  8.8 2.0 copy.59
  10.9 0.0 all-gather.7.cloned.1.call-update
  10.9 0.0 all-reduce.5.cloned.1.call-start
  10.9 0.9 fusion.36
  11.8 0.8 fusion.43
  12.7 15.7 %all-gather = bf16[8,2,4608]{2,1,0:T(2,128)(2,1)S(1)} all-gather(bf16[1,2,4608]{2,1,0:T(2,128)(2,1)S(1)} %fusion.43), channel_id=1, replica_groups=mesh['req'=4,'mlp'=8] {'mlp'}, dimensions={0}, use_global_device_ids=true | all-gather | bytes 165888 | tf_op jit(solution)/shard_map/all_gather | solution.py:75
  28.4 0.1 reshape.185
  28.5 0.0 copy-start.7
  28.5 0.0 copy-start.9
  28.5 0.0 copy-start.10
  28.5 3.1 convolution_convert_fusion.1
  31.6 0.0 copy-done
  31.6 0.4 convolution_convert_fusion.2
  32.0 0.0 copy-start.8
  32.0 2.1 convolution_convert_fusion.3
  34.1 0.0 copy-done.7
  34.2 0.2 convert_reduce_fusion
  34.4 0.0 copy-done.9
  34.4 0.1 select_reduce_fusion
  34.5 0.1 fusion.55
  34.6 0.0 copy-done.10
  34.6 0.2 fusion.64
  34.8 0.2 fusion.63
  35.0 0.1 broadcast_compare_fusion
  35.1 12.1 %all-gather.5.cloned.1.call-done = bf16[4096,256]{0,1:T(8,128)(2,1)} async-done(((bf16[1024,256]{0,1:T(8,128)(2,1)}), bf16[4096,256]{0,1:T(8,128)(2,1)}) %all-gather.5.cloned.1.call-update) | async-done | bytes 2097168 | tf_op jit(solution)/shard_map/all_gather | solution.py:104
  47.3 2.3 fusion.65
  49.5 0.0 copy-start.11
  49.6 0.0 copy-start.5
  49.6 0.0 copy-start.6
  49.6 34.9 %all-gather.7.cloned.1.call-done = bf16[4096,256]{0,1:T(8,128)(2,1)} async-done(((bf16[1024,256]{0,1:T(8,128)(2,1)}), bf16[4096,256]{0,1:T(8,128)(2,1)}) %all-gather.7.cloned.1.call-update) | async-done | bytes 2097168 | tf_op jit(solution)/shard_map/all_gather | solution.py:105
  84.4 2.4 fusion.20
  86.8 0.0 copy-done.8
  86.9 0.2 fusion.13
  87.1 0.2 fusion.14
  87.3 3.7 %convolution_convert_fusion = bf16[16,4608]{1,0:T(8,128)(2,1)} fusion(bf16[16,512]{1,0:T(8,128)(2,1)S(1)} %reshape.183, bf16[512,4608]{1,0:T(8,128)(2,1)} %param.32), kind=kOutput, calls=%fused_computation | convolution fusion | flops 75571200 | bytes 4882432 | tf_op jit(solution)/shard_map/dot_general | solution.py:115
  91.0 0.0 all-reduce.5.cloned.1.call-update
  91.0 0.0 all-reduce.7.cloned.1.call-start
  91.1 0.0 copy-done.11
  91.1 0.6 dynamic-slice
  92.3 51.0 %all-reduce.5.cloned.1.call-done = bf16[16,4608]{1,0:T(8,128)(2,1)} async-done(((bf16[16,4608]{1,0:T(8,128)(2,1)}), bf16[16,4608]{1,0:T(8,128)(2,1)}) %all-reduce.5.cloned.1.call-update) | async-done | bytes 147472
  143.3 1.0 fusion.34
  144.3 0.0 copy-done.3
  144.3 0.0 copy-done.5
  144.4 1.1 multiply_reduce_fusion.1
  145.5 0.0 copy-done.6
  145.5 0.1 fusion.44
  145.6 0.5 copy-done.1
  146.1 44.4 %all-gather.1 = bf16[32,2,4608]{2,1,0:T(2,128)(2,1)S(1)} all-gather(bf16[1,2,4608]{2,1,0:T(2,128)(2,1)S(1)} %fusion.44), channel_id=1, replica_groups=mesh['req'=4,'mlp'=8] {'req','mlp'}, dimensions={0}, use_global_device_ids=true | all-gather | bytes 608256 | tf_op jit(solution)/shard_map/all_gather | solution.py:122
  190.5 0.2 reshape.187
  190.7 7.3 %fusion.66 = f32[64,1152]{1,0:T(8,128)S(1)} fusion(bf16[64,4608]{1,0:T(8,128)(2,1)S(1)} %reshape.187, bf16[1152,4608]{1,0:T(8,128)(2,1)} %param.33), kind=kOutput, calls=%fused_computation.102 | convolution fusion | flops 679477248 | bytes 11501568 | tf_op jit(solution)/shard_map/dot_general | solution.py:123
  198.0 0.0 copy-start.2
  198.0 0.0 copy-start.4
  198.1 13.6 %fusion.19 = f32[64,4608]{1,0:T(8,128)} fusion(bf16[1152,4608]{1,0:T(8,128)(2,1)} %param.35, bf16[64,4608]{1,0:T(8,128)(2,1)S(1)} %reshape.187, bf16[1152,4608]{1,0:T(8,128)(2,1)} %param.34, f32[64,1152]{1,0:T(8,128)S(1)} %fusion.66), kind=kOutput, calls=%fused_computation.29 | convolution fusion | flops 1359691776 | bytes 23298048 | tf_op jit(solution)/shard_map/dot_general | solution.py:127
  211.7 0.0 all-reduce.7.cloned.1.call-update
  211.7 127.5 %all-reduce.7.cloned.1.call-done = f32[64,4608]{1,0:T(8,128)} async-done(((f32[64,4608]{1,0:T(8,128)}), f32[64,4608]{1,0:T(8,128)}) %all-reduce.7.cloned.1.call-update) | async-done | bytes 1179664
  339.2 1.1 multiply_reduce_fusion
  340.2 0.0 copy-done.2
  340.2 0.0 copy-done.4
  340.3 1.6 add_convert_fusion
  (17 shorter events, 0.2 us)
Async XLA Ops:
  6.5 25.0 %copy-start = (bf16[4608,256]{1,0:T(8,128)(2,1)S(1)}, bf16[4608,256]{1,0:T(8,128)(2,1)}, u32[]{:S(2)}) copy-start(bf16[4608,256]{1,0:T(8,128)(2,1)} %param.30) | copy-start | bytes 7077892
  6.5 40.7 %all-gather.5.cloned.1.call-start = ((), (), s32[]{:S(2)}) async-start(), calls=%async_computation | async-start | bytes 2621440 | tf_op jit(solution)/shard_map/all_gather | solution.py:104
  8.8 75.7 %all-gather.7.cloned.1.call-start = ((), (), s32[]{:S(2)}) async-start(), calls=%async_computation.1 | async-start | bytes 2621440 | tf_op jit(solution)/shard_map/all_gather | solution.py:105
  10.9 132.4 %all-reduce.5.cloned.1.call-start = ((), (), s32[]{:S(2)}) async-start(), calls=%async_computation.2 | async-start | bytes 294912
  28.5 5.7 %copy-start.7 = (s32[4,16]{1,0:T(4,128)S(1)}, s32[4,16]{1,0:T(4,128)}, u32[]{:S(2)}) copy-start(s32[4,16]{1,0:T(4,128)} %param.19) | copy-start | bytes 772
  28.5 5.9 %copy-start.9 = (s32[4]{0:T(128)S(1)}, s32[4]{0:T(128)}, u32[]{:S(2)}) copy-start(s32[4]{0:T(128)} %param.20) | copy-start | bytes 52
  28.5 6.1 %copy-start.10 = (bf16[4,256]{1,0:T(4,128)(2,1)S(1)}, bf16[4,256]{1,0:T(4,128)(2,1)}, u32[]{:S(2)}) copy-start(bf16[4,256]{1,0:T(4,128)(2,1)} %param.21) | copy-start | bytes 6148
  32.0 54.9 %copy-start.8 = (bf16[4,256]{1,0:T(4,128)(2,1)S(1)}, bf16[4,256]{1,0:T(4,128)(2,1)}, u32[]{:S(2)}) copy-start(bf16[4,256]{1,0:T(4,128)(2,1)} %param.22) | copy-start | bytes 6148
  49.5 41.5 %copy-start.11 = (u32[32]{0:T(128)S(1)}, u32[32]{0:T(128)}, u32[]{:S(2)}) copy-start(u32[32]{0:T(128)} %constant.81) | copy-start | bytes 388
  49.6 94.8 %copy-start.3 = (bf16[2,4608]{1,0:T(2,128)(2,1)S(1)}, bf16[2,4608]{1,0:T(2,128)(2,1)}, u32[]{:S(2)}) copy-start(bf16[2,4608]{1,0:T(2,128)(2,1)} %param.18) | copy-start | bytes 55300
  49.6 94.8 %copy-start.5 = (f32[4608]{0:T(1024)S(1)}, f32[4608]{0:T(1024)}, u32[]{:S(2)}) copy-start(f32[4608]{0:T(1024)} %param.26) | copy-start | bytes 55300
  49.6 95.9 %copy-start.6 = (f32[4608]{0:T(1024)S(1)}, f32[4608]{0:T(1024)}, u32[]{:S(2)}) copy-start(f32[4608]{0:T(1024)} %param.27) | copy-start | bytes 55300
  91.0 248.1 %all-reduce.7.cloned.1.call-start = ((), (), s32[]{:S(2)}) async-start(), calls=%async_computation.3 | async-start | bytes 2359296
  145.5 0.6 copy-start.1
  198.0 142.2 %copy-start.2 = (f32[2,4608]{1,0:T(2,128)S(1)}, f32[2,4608]{1,0:T(2,128)}, u32[]{:S(2)}) copy-start(f32[2,4608]{1,0:T(2,128)} %copy-done.1) | copy-start | bytes 110596
  198.0 142.2 %copy-start.4 = (f32[4608]{0:T(1024)S(1)}, f32[4608]{0:T(1024)}, u32[]{:S(2)}) copy-start(f32[4608]{0:T(1024)} %param.28) | copy-start | bytes 55300
Sparse Core Ops, SparseCore 0:
  9.2 38.0 all-gather.4
  49.1 35.2 all-gather.6
  91.2 52.0 all-reduce.4
  211.8 127.3 all-reduce.6
where the time goes:
time: 349 us; the launch traced here: 348 us
  waiting for transfers between devices  225 us (64%)
  blocking collectives  60.1 us (17%)
  matrix products  35.6 us (10%)
  between operations  14 us (4%)
  other arithmetic  7.19 us (2%)
  local copies, waits for them, and re-layouts  5.76 us (2%)
    unnamed x6, waiting for transfers between devices  178 us
    all_gather x1, blocking collectives, shards(): piece = lax.all_gather(ffn_in, ('req', 'mlp'), axis=0, tiled=True)  44.4 us
    all_gather x1, waiting for transfers between devices, shards(): lax.all_gather(window_values, 'req', axis=0, tiled=True)  34.9 us
    all_gather x1, blocking collectives, shards(): group_rows = lax.all_gather(normed, 'mlp', axis=0, tiled=True)  15.7 us
    dot_general x1, matrix products, shards(): jnp.dot(hidden, w_down, preferred_element_type=jnp.float32)  13.6 us
    all_gather x1, waiting for transfers between devices, shards(): lax.all_gather(window_keys, 'req', axis=0, tiled=True)  12.1 us
    dot_general x1, matrix products, shards(): lax.dot_general(piece, w_gate, contract, preferred_element_type=jnp.float32)  7.31 us
  transfers between devices with their start and end apart: 4, of which 4 were waited for; matrix products, arithmetic and copies ran while one was open for 4% of the time, Pallas kernels for 0%

commit v1 on v0

--- a/solution.py
+++ b/solution.py
@@ -72,7 +72,12 @@
     local_heads = w_key.shape[1] // HD
     token_float = tokens.astype(jnp.float32)
     normed = (rms_scale(token_float) * attn_gain).astype(jnp.bfloat16)
-    group_rows = lax.all_gather(normed, "mlp", axis=0, tiled=True)
+    ring = [normed]
+    for hop in range(7):
+        ring.append(lax.ppermute(ring[-1], "mlp", [(dev, (dev + 1) % 8) for dev in range(8)]))
+    group_rows = jnp.roll(
+        jnp.concatenate(ring[::-1], axis=0), (lax.axis_index("mlp") + 1) * ring[0].shape[0], axis=0
+    )
     query_rows = (
         jnp.dot(group_rows, w_query, preferred_element_type=jnp.float32)
         .astype(jnp.bfloat16)

time: 349 us -> 349 us (level)
  blocking collectives: 60.1 us -> 44.4 us
  waiting for transfers between devices: 225 us -> 238 us
    ppermute x0 -> x7, waiting for transfers between devices: none -> 30.4 us  [shards(): lax.ppermute(ring[-1], 'mlp', [(dev, (dev + 1) % 8) for dev in range(8)])]
    all_gather x1 -> x0, blocking collectives: 15.7 us -> none  [shards(): group_rows = lax.all_gather(normed, 'mlp', axis=0, tiled=True)]
    all_gather x1, waiting for transfers between devices: 12.1 us -> 0.02 us  [shards(): lax.all_gather(window_keys, 'req', axis=0, tiled=True)]
    all_gather x1, waiting for transfers between devices: 34.9 us -> 29.2 us  [shards(): lax.all_gather(window_values, 'req', axis=0, tiled=True)]
  transfers between devices with their start and end apart: 4 -> 11, of which waited for: 4 -> 10; matrix products, arithmetic and copies ran while one was open for 4% -> 5% of each run, Pallas kernels for 0% -> 0%
where the time goes in v1:
time: 349 us
  waiting for transfers between devices  238 us (68%)
  blocking collectives  44.4 us (13%)
  matrix products  35.7 us (10%)
  between operations  14 us (4%)
  other arithmetic  8.61 us (2%)
  local copies, waits for them, and re-layouts  6.8 us (2%)
    unnamed x6, waiting for transfers between devices  179 us
    all_gather x1, blocking collectives, shards(): piece = lax.all_gather(ffn_in, ('req', 'mlp'), axis=0, tiled=True)  44.4 us
    ppermute x7, waiting for transfers between devices, shards(): lax.ppermute(ring[-1], 'mlp', [(dev, (dev + 1) % 8) for dev in range(8)])  30.4 us
    all_gather x1, waiting for transfers between devices, shards(): lax.all_gather(window_values, 'req', axis=0, tiled=True)  29.2 us
    dot_general x1, matrix products, shards(): jnp.dot(hidden, w_down, preferred_element_type=jnp.float32)  13.6 us
    dot_general x1, matrix products, shards(): lax.dot_general(piece, w_gate, contract, preferred_element_type=jnp.float32)  7.32 us
  transfers between devices with their start and end apart: 11, of which 10 were waited for; matrix products, arithmetic and copies ran while one was open for 5% of the time, Pallas kernels for 0%

profile of v1, /device:TPU:0, one launch (start us, length us, event | category | flops | bytes accessed | tf_op | source)
XLA Modules:
  0.0 348.5 jit_solution(3159331643518075505)
XLA Ops:
  6.5 0.0 copy-start
  6.5 0.0 all-gather.4.cloned.1.call-start
  6.5 2.2 copy.56
  8.8 0.0 all-gather.4.cloned.1.call-update
  8.8 0.0 all-gather.6.cloned.1.call-start
  8.8 0.9 fusion.39
  9.7 0.8 fusion.41
  10.5 0.5 collective-permute-start
  11.1 2.0 copy.59
  13.1 0.0 all-gather.6.cloned.1.call-update
  13.1 0.0 all-reduce.5.cloned.1.call-start
  13.2 0.8 select_reduce_fusion
  14.0 2.6 collective-permute-done
  16.5 0.2 collective-permute-start.1
  16.7 4.8 %collective-permute-done.1 = bf16[2,4608]{1,0:T(2,128)(2,1)S(1)} collective-permute-done((bf16[2,4608]{1,0:T(2,128)(2,1)S(1)}, bf16[2,4608]{1,0:T(2,128)(2,1)S(1)}, u32[]{:S(2)}, u32[]{:S(2)}) %collective-permute-start.1) | collective-permute-done | bytes 18464 | tf_op jit(solution)/shard_map/ppermute | solution.py:77
  21.5 0.0 collective-permute-start.2
  21.5 1.0 convert_reduce_fusion
  22.5 4.0 %collective-permute-done.2 = bf16[2,4608]{1,0:T(2,128)(2,1)S(1)} collective-permute-done((bf16[2,4608]{1,0:T(2,128)(2,1)S(1)}, bf16[2,4608]{1,0:T(2,128)(2,1)S(1)}, u32[]{:S(2)}, u32[]{:S(2)}) %collective-permute-start.2) | collective-permute-done | bytes 18464 | tf_op jit(solution)/shard_map/ppermute | solution.py:77
  26.5 0.0 collective-permute-start.3
  26.5 5.0 %collective-permute-done.3 = bf16[2,4608]{1,0:T(2,128)(2,1)S(1)} collective-permute-done((bf16[2,4608]{1,0:T(2,128)(2,1)S(1)}, bf16[2,4608]{1,0:T(2,128)(2,1)S(1)}, u32[]{:S(2)}, u32[]{:S(2)}) %collective-permute-start.3) | collective-permute-done | bytes 18464 | tf_op jit(solution)/shard_map/ppermute | solution.py:77
  31.5 0.0 collective-permute-start.4
  31.5 0.1 broadcast_compare_fusion
  31.6 4.9 %collective-permute-done.4 = bf16[2,4608]{1,0:T(2,128)(2,1)S(1)} collective-permute-done((bf16[2,4608]{1,0:T(2,128)(2,1)S(1)}, bf16[2,4608]{1,0:T(2,128)(2,1)S(1)}, u32[]{:S(2)}, u32[]{:S(2)}) %collective-permute-start.4) | collective-permute-done | bytes 18464 | tf_op jit(solution)/shard_map/ppermute | solution.py:77
  36.5 0.0 collective-permute-start.5
  36.5 0.7 fusion.65
  37.2 4.3 %collective-permute-done.5 = bf16[2,4608]{1,0:T(2,128)(2,1)S(1)} collective-permute-done((bf16[2,4608]{1,0:T(2,128)(2,1)S(1)}, bf16[2,4608]{1,0:T(2,128)(2,1)S(1)}, u32[]{:S(2)}, u32[]{:S(2)}) %collective-permute-start.5) | collective-permute-done | bytes 18464 | tf_op jit(solution)/shard_map/ppermute | solution.py:77
  41.5 0.0 collective-permute-start.6
  41.5 0.1 fusion.57
  41.5 4.9 %collective-permute-done.6 = bf16[2,4608]{1,0:T(2,128)(2,1)S(1)} collective-permute-done((bf16[2,4608]{1,0:T(2,128)(2,1)S(1)}, bf16[2,4608]{1,0:T(2,128)(2,1)S(1)}, u32[]{:S(2)}, u32[]{:S(2)}) %collective-permute-start.6) | collective-permute-done | bytes 18464 | tf_op jit(solution)/shard_map/ppermute | solution.py:77
  46.4 0.4 concatenate.6
  46.9 0.0 copy-start.8
  46.9 0.4 convolution_convert_fusion.3
  47.4 3.1 convolution_convert_fusion.1
  50.4 2.1 convolution_convert_fusion.2
  52.5 0.2 fusion.71
  52.7 0.2 fusion.70
  52.9 0.0 all-gather.4.cloned.1.call-done
  53.0 2.3 fusion.72
  55.3 0.0 copy-start.5
  55.3 0.0 copy-start.6
  55.3 29.2 %all-gather.6.cloned.1.call-done = bf16[4096,256]{0,1:T(8,128)(2,1)} async-done(((bf16[1024,256]{0,1:T(8,128)(2,1)}), bf16[4096,256]{0,1:T(8,128)(2,1)}) %all-gather.6.cloned.1.call-update) | async-done | bytes 2097168 | tf_op jit(solution)/shard_map/all_gather | solution.py:110
  84.5 2.4 fusion.20
  86.9 0.2 fusion.13
  87.1 0.2 fusion.14
  87.3 3.7 %convolution_convert_fusion = bf16[16,4608]{1,0:T(8,128)(2,1)} fusion(bf16[16,512]{1,0:T(8,128)(2,1)S(1)} %reshape.183, bf16[512,4608]{1,0:T(8,128)(2,1)} %param.32), kind=kOutput, calls=%fused_computation | convolution fusion | flops 75571200 | bytes 4882432 | tf_op jit(solution)/shard_map/dot_general | solution.py:120
  91.0 0.0 all-reduce.5.cloned.1.call-update
  91.1 0.0 all-reduce.7.cloned.1.call-start
  91.1 0.0 copy-done.9
  91.1 0.6 dynamic-slice
  92.4 51.0 %all-reduce.5.cloned.1.call-done = bf16[16,4608]{1,0:T(8,128)(2,1)} async-done(((bf16[16,4608]{1,0:T(8,128)(2,1)}), bf16[16,4608]{1,0:T(8,128)(2,1)}) %all-reduce.5.cloned.1.call-update) | async-done | bytes 147472
  143.3 1.0 fusion.37
  144.4 1.1 multiply_reduce_fusion.1
  145.5 0.1 fusion.46
  145.6 0.5 copy-done.1
  146.1 44.4 %all-gather = bf16[32,2,4608]{2,1,0:T(2,128)(2,1)S(1)} all-gather(bf16[1,2,4608]{2,1,0:T(2,128)(2,1)S(1)} %fusion.46), channel_id=1, replica_groups=mesh['req'=4,'mlp'=8] {'req','mlp'}, dimensions={0}, use_global_device_ids=true | all-gather | bytes 608256 | tf_op jit(solution)/shard_map/all_gather | solution.py:127
  190.5 0.2 reshape.185
  190.7 7.3 %fusion.73 = f32[64,1152]{1,0:T(8,128)S(1)} fusion(bf16[64,4608]{1,0:T(8,128)(2,1)S(1)} %reshape.185, bf16[1152,4608]{1,0:T(8,128)(2,1)} %param.33), kind=kOutput, calls=%fused_computation.109 | convolution fusion | flops 679477248 | bytes 11501568 | tf_op jit(solution)/shard_map/dot_general | solution.py:128
  198.1 0.0 copy-start.4
  198.1 13.6 %fusion.19 = f32[64,4608]{1,0:T(8,128)} fusion(bf16[1152,4608]{1,0:T(8,128)(2,1)} %param.35, bf16[64,4608]{1,0:T(8,128)(2,1)S(1)} %reshape.185, bf16[1152,4608]{1,0:T(8,128)(2,1)} %param.34, f32[64,1152]{1,0:T(8,128)S(1)} %fusion.73), kind=kOutput, calls=%fused_computation.29 | convolution fusion | flops 1359691776 | bytes 23298048 | tf_op jit(solution)/shard_map/dot_general | solution.py:132
  211.7 0.0 all-reduce.7.cloned.1.call-update
  211.7 127.6 %all-reduce.7.cloned.1.call-done = f32[64,4608]{1,0:T(8,128)} async-done(((f32[64,4608]{1,0:T(8,128)}), f32[64,4608]{1,0:T(8,128)}) %all-reduce.7.cloned.1.call-update) | async-done | bytes 1179664
  339.3 1.1 multiply_reduce_fusion
  340.3 0.0 copy-done.4
  340.4 1.6 add_convert_fusion
  (26 shorter events, 0.2 us)
Async XLA Ops:
  6.5 40.4 %copy-start = (bf16[4608,256]{1,0:T(8,128)(2,1)S(1)}, bf16[4608,256]{1,0:T(8,128)(2,1)}, u32[]{:S(2)}) copy-start(bf16[4608,256]{1,0:T(8,128)(2,1)} %param.31) | copy-start | bytes 7077892
  6.5 46.4 %all-gather.4.cloned.1.call-start = ((), (), s32[]{:S(2)}) async-start(), calls=%async_computation | async-start | bytes 2621440 | tf_op jit(solution)/shard_map/all_gather | solution.py:109
  8.8 75.7 %all-gather.6.cloned.1.call-start = ((), (), s32[]{:S(2)}) async-start(), calls=%async_computation.1 | async-start | bytes 2621440 | tf_op jit(solution)/shard_map/all_gather | solution.py:110
  10.5 6.0 %collective-permute-start = (bf16[2,4608]{1,0:T(2,128)(2,1)S(1)}, bf16[2,4608]{1,0:T(2,128)(2,1)S(1)}, u32[]{:S(2)}, u32[]{:S(2)}) collective-permute-start(bf16[2,4608]{1,0:T(2,128)(2,1)S(1)} %fusion.41), channel_id=1, source_target_pairs={{0,1},{1,2},{2,3},{3,4},{4,5},{5,6},{6,7},{7,0},{8,9},{9,10},{10,1... | collective-permute-start | bytes 55304 | tf_op jit(solution)/shard_map/ppermute | solution.py:77
  13.1 130.2 %all-reduce.5.cloned.1.call-start = ((), (), s32[]{:S(2)}) async-start(), calls=%async_computation.2 | async-start | bytes 294912
  16.5 5.0 %collective-permute-start.1 = (bf16[2,4608]{1,0:T(2,128)(2,1)S(1)}, bf16[2,4608]{1,0:T(2,128)(2,1)S(1)}, u32[]{:S(2)}, u32[]{:S(2)}) collective-permute-start(bf16[2,4608]{1,0:T(2,128)(2,1)S(1)} %collective-permute-done), channel_id=1, source_target_pairs={{0,1},{1,2},{2,3},{3,4},{4,5},{5,6},{6,7},{7,0},{8,9},{9,10},{10,1... | collective-permute-start | bytes 55304 | tf_op jit(solution)/shard_map/ppermute | solution.py:77
  21.5 5.0 %collective-permute-start.2 = (bf16[2,4608]{1,0:T(2,128)(2,1)S(1)}, bf16[2,4608]{1,0:T(2,128)(2,1)S(1)}, u32[]{:S(2)}, u32[]{:S(2)}) collective-permute-start(bf16[2,4608]{1,0:T(2,128)(2,1)S(1)} %collective-permute-done.1), channel_id=1, source_target_pairs={{0,1},{1,2},{2,3},{3,4},{4,5},{5,6},{6,7},{7,0},{8,9},{9,10},{10,1... | collective-permute-start | bytes 55304 | tf_op jit(solution)/shard_map/ppermute | solution.py:77
  26.5 5.0 %collective-permute-start.3 = (bf16[2,4608]{1,0:T(2,128)(2,1)S(1)}, bf16[2,4608]{1,0:T(2,128)(2,1)S(1)}, u32[]{:S(2)}, u32[]{:S(2)}) collective-permute-start(bf16[2,4608]{1,0:T(2,128)(2,1)S(1)} %collective-permute-done.2), channel_id=1, source_target_pairs={{0,1},{1,2},{2,3},{3,4},{4,5},{5,6},{6,7},{7,0},{8,9},{9,10},{10,1... | collective-permute-start | bytes 55304 | tf_op jit(solution)/shard_map/ppermute | solution.py:77
  31.5 5.0 %collective-permute-start.4 = (bf16[2,4608]{1,0:T(2,128)(2,1)S(1)}, bf16[2,4608]{1,0:T(2,128)(2,1)S(1)}, u32[]{:S(2)}, u32[]{:S(2)}) collective-permute-start(bf16[2,4608]{1,0:T(2,128)(2,1)S(1)} %collective-permute-done.3), channel_id=1, source_target_pairs={{0,1},{1,2},{2,3},{3,4},{4,5},{5,6},{6,7},{7,0},{8,9},{9,10},{10,1... | collective-permute-start | bytes 55304 | tf_op jit(solution)/shard_map/ppermute | solution.py:77
  36.5 5.0 %collective-permute-start.5 = (bf16[2,4608]{1,0:T(2,128)(2,1)S(1)}, bf16[2,4608]{1,0:T(2,128)(2,1)S(1)}, u32[]{:S(2)}, u32[]{:S(2)}) collective-permute-start(bf16[2,4608]{1,0:T(2,128)(2,1)S(1)} %collective-permute-done.4), channel_id=1, source_target_pairs={{0,1},{1,2},{2,3},{3,4},{4,5},{5,6},{6,7},{7,0},{8,9},{9,10},{10,1... | collective-permute-start | bytes 55304 | tf_op jit(solution)/shard_map/ppermute | solution.py:77
  41.5 5.0 %collective-permute-start.6 = (bf16[2,4608]{1,0:T(2,128)(2,1)S(1)}, bf16[2,4608]{1,0:T(2,128)(2,1)S(1)}, u32[]{:S(2)}, u32[]{:S(2)}) collective-permute-start(bf16[2,4608]{1,0:T(2,128)(2,1)S(1)} %collective-permute-done.5), channel_id=1, source_target_pairs={{0,1},{1,2},{2,3},{3,4},{4,5},{5,6},{6,7},{7,0},{8,9},{9,10},{10,1... | collective-permute-start | bytes 55304 | tf_op jit(solution)/shard_map/ppermute | solution.py:77
  46.9 5.6 %copy-start.8 = (bf16[4,256]{1,0:T(4,128)(2,1)S(1)}, bf16[4,256]{1,0:T(4,128)(2,1)}, u32[]{:S(2)}) copy-start(bf16[4,256]{1,0:T(4,128)(2,1)} %param.21) | copy-start | bytes 6148
  50.4 36.5 %copy-start.7 = (bf16[4,256]{1,0:T(4,128)(2,1)S(1)}, bf16[4,256]{1,0:T(4,128)(2,1)}, u32[]{:S(2)}) copy-start(bf16[4,256]{1,0:T(4,128)(2,1)} %param.22) | copy-start | bytes 6148
  55.2 35.9 %copy-start.9 = (u32[32]{0:T(128)S(1)}, u32[32]{0:T(128)}, u32[]{:S(2)}) copy-start(u32[32]{0:T(128)} %constant.108) | copy-start | bytes 388
  55.3 89.1 %copy-start.3 = (bf16[2,4608]{1,0:T(2,128)(2,1)S(1)}, bf16[2,4608]{1,0:T(2,128)(2,1)}, u32[]{:S(2)}) copy-start(bf16[2,4608]{1,0:T(2,128)(2,1)} %param.18) | copy-start | bytes 55300
  55.3 89.1 %copy-start.5 = (f32[4608]{0:T(1024)S(1)}, f32[4608]{0:T(1024)}, u32[]{:S(2)}) copy-start(f32[4608]{0:T(1024)} %param.26) | copy-start | bytes 55300
  55.3 90.2 %copy-start.6 = (f32[4608]{0:T(1024)S(1)}, f32[4608]{0:T(1024)}, u32[]{:S(2)}) copy-start(f32[4608]{0:T(1024)} %param.27) | copy-start | bytes 55300
  91.1 248.2 %all-reduce.7.cloned.1.call-start = ((), (), s32[]{:S(2)}) async-start(), calls=%async_computation.3 | async-start | bytes 2359296
  145.5 0.6 copy-start.1
  198.0 142.3 %copy-start.2 = (f32[2,4608]{1,0:T(2,128)S(1)}, f32[2,4608]{1,0:T(2,128)}, u32[]{:S(2)}) copy-start(f32[2,4608]{1,0:T(2,128)} %copy-done.1) | copy-start | bytes 110596
  198.1 142.3 %copy-start.4 = (f32[4608]{0:T(1024)S(1)}, f32[4608]{0:T(1024)}, u32[]{:S(2)}) copy-start(f32[4608]{0:T(1024)} %param.28) | copy-start | bytes 55300
Sparse Core Ops, SparseCore 0:
  9.2 38.0 all-gather.3
  49.1 35.2 all-gather.5
  91.2 52.0 all-reduce.4
  211.8 127.3 all-reduce.6
